TPU v7x, 32 devices: a whole 2x2x4 slice. The times are simulated.
32 devices in a mesh: grp: 2 (over x), seq: 8 (over z, y), mdl: 2 (over core).
Axes of the slice: x: 2, y: 2, z: 4, core: 2. Of those that a mesh axis runs over, the one named last changes fastest.
Arguments:
- signal: float32 [8, 128, 8192], P('grp', 'mdl', 'seq'), parts along dimension 0, may hold values from -6 to 6
- lengths: int32 [8], P('grp'), parts along dimension 0, may hold values from 1 to 64, 160 in all
- chan_weight: bfloat16 [128, 128, 16], P('mdl'), may hold values from -0.5 to 0.5
- up_weight: bfloat16 [4, 2048, 4096], P(None, 'seq', 'mdl'), may hold values from -0.125 to 0.125
- down_weight: bfloat16 [4, 2048, 4096], P(None, 'seq', 'mdl'), may hold values from -0.09375 to 0.09375
Outputs:
- features: bfloat16 [8, 64, 2048], P(('grp', 'mdl'), 'seq'), parts along dimension 0
There are 2 independent parts, one for each index of `grp`. A program takes and returns all parts, laid end to end along the dimension named above; an argument that names none is the same for every part. Nothing has to cross between parts.
Inputs may be any that keep to these rules, and one draw needn't show every extreme that they name: `lengths`: live windows of each recording; one recording is live for all 64, and all recordings together have (320) // 2.
All inputs are finite; a program needn't handle non-finite values.
Results may differ from a plain program's by a relative error of at most 0.014.
Values may be sent and summed in bfloat16 or wider, within the bound.
A program may use at most 128 MiB of HBM per device.

v0:
```python
import math
import jax
import jax.numpy as jnp
from jax import lax
from jax.sharding import PartitionSpec as P

HOP = 128
EPSILON = 1e-06


def shifted(x, axis, by):
    size = lax.axis_size(axis)
    pairs = [(i, i + by) for i in range(size) if 0 <= i + by < size]
    return lax.ppermute(x, axis, pairs)


def spectral_table(half_span):
    full_span = 2 * half_span
    row_index = jnp.arange(full_span, dtype=jnp.int32)
    col_index = jnp.arange(half_span, dtype=jnp.int32)
    phases = row_index[:, None] * col_index[None, :] % full_span
    angles = phases.astype(jnp.float32) * (2.0 * math.pi / full_span)
    window_taper = 0.5 - 0.5 * jnp.cos(row_index.astype(jnp.float32) * (2.0 * math.pi / full_span))
    weighting = window_taper * (1.0 / math.sqrt(full_span))
    joined = jnp.concatenate([jnp.cos(angles), -jnp.sin(angles)], axis=1) * weighting[:, None]
    return jnp.concatenate([joined[:half_span], joined[half_span:]], axis=1)


def log_power(spectrum):
    half_span = spectrum.shape[-1] // 2
    real_part = spectrum[..., :half_span]
    imag_part = spectrum[..., half_span:]
    return jnp.log1p(real_part * real_part + imag_part * imag_part).astype(jnp.bfloat16)


def project_down(hidden, own_down):
    return lax.dot_general(
        hidden, own_down, (((1,), (1,)), ((), ())), preferred_element_type=jnp.float32
    )


def apply_layer(state, up_rows, down_rows, width):
    values = state.astype(jnp.float32)
    squares = lax.psum(jnp.sum(values * values, axis=1, keepdims=True), "seq")
    partial = jnp.dot(state, up_rows, preferred_element_type=jnp.float32).astype(jnp.bfloat16)
    summed = lax.psum_scatter(partial, "seq", scatter_dimension=1, tiled=True)
    scale = lax.rsqrt(squares * (1.0 / width) + EPSILON)
    hidden = jax.nn.gelu(summed.astype(jnp.float32) * scale).astype(jnp.bfloat16)
    hidden = lax.all_gather(hidden, "seq", axis=1, tiled=True)
    added = lax.psum(project_down(hidden, down_rows), "mdl")
    return (values + added).astype(jnp.bfloat16)


def body(signal, lengths, chan_weight, up_weight, down_weight):
    streams, channels, samples = signal.shape
    frames = samples // HOP
    dft_table = spectral_table(HOP)
    boundary = shifted(signal[:, :, :HOP], "seq", -1)
    local_part = jnp.dot(
        signal.reshape(streams, channels, frames, HOP), dft_table, precision=lax.Precision.HIGHEST
    )
    edge_part = jnp.dot(boundary, dft_table[:, 2 * HOP :], precision=lax.Precision.HIGHEST)
    following = jnp.concatenate([local_part[:, :, 1:, 2 * HOP :], edge_part[:, :, None, :]], axis=2)
    spectrum = local_part[..., : 2 * HOP] + following
    logpower = log_power(spectrum)
    embedded = jnp.einsum(
        "scfb,cbe->sfce", logpower, chan_weight, preferred_element_type=jnp.float32
    )
    embedded = embedded.reshape(streams, frames, channels * chan_weight.shape[2])
    frame_index = lax.axis_index("seq") * frames + jnp.arange(frames, dtype=jnp.int32)
    live_mask = frame_index[None, :] < lengths[:, None]
    tokens = jnp.where(live_mask[:, :, None], embedded, 0.0).astype(jnp.bfloat16)
    rows = lax.all_gather(tokens.reshape(streams * frames, -1), "mdl", axis=1, tiled=True)
    state = lax.all_to_all(rows, "seq", split_axis=1, concat_axis=0, tiled=True)
    width = rows.shape[1]
    for layer in range(up_weight.shape[0]):
        state = apply_layer(state, up_weight[layer], down_weight[layer], width)
    rows = lax.all_to_all(state, "seq", split_axis=0, concat_axis=1, tiled=True)
    full_rows = rows.reshape(streams, frames, width)
    half_streams = streams // lax.axis_size("mdl")
    return lax.dynamic_slice_in_dim(
        full_rows, lax.axis_index("mdl") * half_streams, half_streams, 0
    )


def solution(mesh):
    return jax.shard_map(
        body,
        mesh=mesh,
        in_specs=(
            P("grp", "mdl", "seq"),
            P("grp"),
            P("mdl", None, None),
            P(None, "seq", "mdl"),
            P(None, "seq", "mdl"),
        ),
        out_specs=P(("grp", "mdl"), "seq", None),
        check_vma=False,
    )
```

profile of v0, /device:TPU:0, one launch (start us, length us, event | category | flops | bytes accessed | tf_op | source)
XLA Modules:
  0.0 576.4 jit_solution(18243975974515709880)
XLA Ops:
  9.5 4.7 convolution_bitcast_fusion
  22.9 15.4 %all_to_all.35 = bf16[32,8,256]{2,0,1:T(8,128)(2,1)S(1)} all-to-all(bf16[32,8,256]{2,0,1:T(8,128)(2,1)S(1)} %bitcast.87), channel_id=1, replica_groups=mesh['grp'=2,'seq'=8,'mdl'=2] {'seq'}, dimensions={1} | all-to-all | bytes 262144 | tf_op jit(solution)/shard_map/all_to_all | solution.py:74
  41.3 18.6 %psum.56 = f32[256,1]{0,1:T(1,128)S(1)} all-reduce(f32[256,1]{0,1:T(1,128)S(1)} %broadcast_in_dim.36), channel_id=1, replica_groups=mesh['grp'=2,'seq'=8,'mdl'=2] {'seq'}, use_global_device_ids=true, to_apply=%region_2.3 | all-reduce | flops 256 | bytes 2048 | tf_op jit(solution)/shard_map/psum | solution.py:44
  59.9 43.4 %reduce-scatter.5.cloned.1.call-done = bf16[256,256]{1,0:T(8,128)(2,1)} async-done(((bf16[256,2048]{1,0:T(8,128)(2,1)}), bf16[256,256]{1,0:T(8,128)(2,1)}) %reduce-scatter.5.cloned.1.call-update) | async-done | bytes 131088 | tf_op jit(solution)/shard_map/reduce_scatter | solution.py:46
  105.0 39.1 %all-gather.5.cloned.1.call-done = bf16[256,2048]{1,0:T(8,128)(2,1)} async-done(((bf16[256,256]{1,0:T(8,128)(2,1)}), bf16[256,2048]{1,0:T(8,128)(2,1)}) %all-gather.5.cloned.1.call-update) | async-done | bytes 1048592 | tf_op jit(solution)/shard_map/all_gather | solution.py:49
  144.1 2.7 fusion.14
  146.9 17.3 %all-reduce.5.cloned.1.call-done = f32[256,256]{1,0:T(8,128)} async-done(((f32[256,256]{1,0:T(8,128)}), f32[256,256]{1,0:T(8,128)}) %all-reduce.5.cloned.1.call-update) | async-done | bytes 262160 | tf_op jit(solution)/shard_map/psum | solution.py:50
  168.0 21.7 %psum.58 = f32[256,1]{0,1:T(1,128)S(1)} all-reduce(f32[256,1]{0,1:T(1,128)S(1)} %bitcast.88), channel_id=1, replica_groups=mesh['grp'=2,'seq'=8,'mdl'=2] {'seq'}, use_global_device_ids=true, to_apply=%region_6.7 | all-reduce | flops 256 | bytes 2048 | tf_op jit(solution)/shard_map/psum | solution.py:44
  189.7 43.6 %reduce-scatter.7.cloned.1.call-done = bf16[256,256]{1,0:T(8,128)(2,1)} async-done(((bf16[256,2048]{1,0:T(8,128)(2,1)}), bf16[256,256]{1,0:T(8,128)(2,1)}) %reduce-scatter.7.cloned.1.call-update) | async-done | bytes 131088 | tf_op jit(solution)/shard_map/reduce_scatter | solution.py:46
  235.1 38.8 %all-gather.7.cloned.1.call-done = bf16[256,2048]{1,0:T(8,128)(2,1)} async-done(((bf16[256,256]{1,0:T(8,128)(2,1)}), bf16[256,2048]{1,0:T(8,128)(2,1)}) %all-gather.7.cloned.1.call-update) | async-done | bytes 1048592 | tf_op jit(solution)/shard_map/all_gather | solution.py:49
  273.9 2.7 fusion.11
  276.7 17.3 %all-reduce.7.cloned.1.call-done = f32[256,256]{1,0:T(8,128)} async-done(((f32[256,256]{1,0:T(8,128)}), f32[256,256]{1,0:T(8,128)}) %all-reduce.7.cloned.1.call-update) | async-done | bytes 262160 | tf_op jit(solution)/shard_map/psum | solution.py:50
  297.8 21.7 %psum.60 = f32[256,1]{0,1:T(1,128)S(1)} all-reduce(f32[256,1]{0,1:T(1,128)S(1)} %bitcast.89), channel_id=1, replica_groups=mesh['grp'=2,'seq'=8,'mdl'=2] {'seq'}, use_global_device_ids=true, to_apply=%region_10.11 | all-reduce | flops 256 | bytes 2048 | tf_op jit(solution)/shard_map/psum | solution.py:44
  319.5 43.6 %reduce-scatter.9.cloned.1.call-done = bf16[256,256]{1,0:T(8,128)(2,1)} async-done(((bf16[256,2048]{1,0:T(8,128)(2,1)}), bf16[256,256]{1,0:T(8,128)(2,1)}) %reduce-scatter.9.cloned.1.call-update) | async-done | bytes 131088 | tf_op jit(solution)/shard_map/reduce_scatter | solution.py:46
  364.9 39.0 %all-gather.9.cloned.1.call-done = bf16[256,2048]{1,0:T(8,128)(2,1)} async-done(((bf16[256,256]{1,0:T(8,128)(2,1)}), bf16[256,2048]{1,0:T(8,128)(2,1)}) %all-gather.9.cloned.1.call-update) | async-done | bytes 1048592 | tf_op jit(solution)/shard_map/all_gather | solution.py:49
  403.9 2.7 fusion.8
  406.7 17.3 %all-reduce.9.cloned.1.call-done = f32[256,256]{1,0:T(8,128)} async-done(((f32[256,256]{1,0:T(8,128)}), f32[256,256]{1,0:T(8,128)}) %all-reduce.9.cloned.1.call-update) | async-done | bytes 262160 | tf_op jit(solution)/shard_map/psum | solution.py:50
  427.7 21.7 %psum.62 = f32[256,1]{0,1:T(1,128)S(1)} all-reduce(f32[256,1]{0,1:T(1,128)S(1)} %bitcast.90), channel_id=1, replica_groups=mesh['grp'=2,'seq'=8,'mdl'=2] {'seq'}, use_global_device_ids=true, to_apply=%region_14.15 | all-reduce | flops 256 | bytes 2048 | tf_op jit(solution)/shard_map/psum | solution.py:44
  449.4 43.6 %reduce-scatter.11.cloned.1.call-done = bf16[256,256]{1,0:T(8,128)(2,1)} async-done(((bf16[256,2048]{1,0:T(8,128)(2,1)}), bf16[256,256]{1,0:T(8,128)(2,1)}) %reduce-scatter.11.cloned.1.call-update) | async-done | bytes 131088 | tf_op jit(solution)/shard_map/reduce_scatter | solution.py:46
  494.8 39.0 %all-gather.11.cloned.1.call-done = bf16[256,2048]{1,0:T(8,128)(2,1)} async-done(((bf16[256,256]{1,0:T(8,128)(2,1)}), bf16[256,2048]{1,0:T(8,128)(2,1)}) %all-gather.11.cloned.1.call-update) | async-done | bytes 1048592 | tf_op jit(solution)/shard_map/all_gather | solution.py:49
  533.8 2.7 fusion.5
  536.6 17.3 %all-reduce.11.cloned.1.call-done = f32[256,256]{1,0:T(8,128)} async-done(((f32[256,256]{1,0:T(8,128)}), f32[256,256]{1,0:T(8,128)}) %all-reduce.11.cloned.1.call-update) | async-done | bytes 262160 | tf_op jit(solution)/shard_map/psum | solution.py:50
  555.5 5.8 %all-to-all-start.1 = ((bf16[8,32,256]{2,1,0:T(8,128)(2,1)}), bf16[8,32,256]{2,1,0:T(8,128)(2,1)S(1)}, u32[]{:S(2)}, u32[]{:S(2)}) async-start(bf16[8,32,256]{2,1,0:T(8,128)(2,1)} %bitcast.27), calls=%async_computation.5 | async-start | bytes 262144 | tf_op jit(solution)/shard_map/all_to_all | solution.py:78
  561.3 7.4 %all-to-all-done.1 = bf16[8,32,256]{2,1,0:T(8,128)(2,1)S(1)} async-done(((bf16[8,32,256]{2,1,0:T(8,128)(2,1)}), bf16[8,32,256]{2,1,0:T(8,128)(2,1)S(1)}, u32[]{:S(2)}, u32[]{:S(2)}) %all-to-all-start.1) | async-done | bytes 131104 | tf_op jit(solution)/shard_map/all_to_all | solution.py:78
  (74 shorter events, 35.6 us)
Async XLA Ops:
  6.5 12.9 %copy-start = (bf16[64,128,16]{1,2,0:T(8,128)(2,1)S(1)}, bf16[64,128,16]{1,2,0:T(8,128)(2,1)}, u32[]{:S(2)}) copy-start(bf16[64,128,16]{1,2,0:T(8,128)(2,1)} %param.7) | copy-start | bytes 786436
  6.5 96.7 %reduce-scatter.5.cloned.1.call-start = ((), (), s32[]{:S(2)}) async-start(), calls=%async_computation.6 | async-start | bytes 1179648 | tf_op jit(solution)/shard_map/reduce_scatter | solution.py:46
  7.5 9.2 %collective-permute-start = (f32[4,64,128]{2,1,0:T(8,128)S(1)}, f32[4,64,128]{2,1,0:T(8,128)S(1)}, u32[]{:S(2)}, u32[]{:S(2)}) collective-permute-start(f32[4,64,128]{2,1,0:T(8,128)S(1)} %slice.49), channel_id=1, source_target_pairs={{2,0},{4,2},{6,4},{8,6},{10,8},{12,10},{14,12},{3,1},{5,3},{7,5},{... | collective-permute-start | bytes 393224 | tf_op jit(solution)/shard_map/ppermute | solution.py:14
  9.5 7.0 %copy-start.2 = (s32[4]{0:T(128)S(1)}, s32[4]{0:T(128)}, u32[]{:S(2)}) copy-start(s32[4]{0:T(128)} %param.6) | copy-start | bytes 52
  14.3 1.9 copy-start.1
  41.0 103.1 %all-gather.5.cloned.1.call-start = ((), (), s32[]{:S(2)}) async-start(), calls=%async_computation.7 | async-start | bytes 1179648 | tf_op jit(solution)/shard_map/all_gather | solution.py:49
  105.0 59.2 %all-reduce.5.cloned.1.call-start = ((), (), s32[]{:S(2)}) async-start(), calls=%async_computation.8 | async-start | bytes 524288 | tf_op jit(solution)/shard_map/psum | solution.py:50
  146.9 86.4 %reduce-scatter.7.cloned.1.call-start = ((), (), s32[]{:S(2)}) async-start(), calls=%async_computation.9 | async-start | bytes 1179648 | tf_op jit(solution)/shard_map/reduce_scatter | solution.py:46
  167.9 106.0 %all-gather.7.cloned.1.call-start = ((), (), s32[]{:S(2)}) async-start(), calls=%async_computation.10 | async-start | bytes 1179648 | tf_op jit(solution)/shard_map/all_gather | solution.py:49
  235.0 59.0 %all-reduce.7.cloned.1.call-start = ((), (), s32[]{:S(2)}) async-start(), calls=%async_computation.11 | async-start | bytes 524288 | tf_op jit(solution)/shard_map/psum | solution.py:50
  276.7 86.4 %reduce-scatter.9.cloned.1.call-start = ((), (), s32[]{:S(2)}) async-start(), calls=%async_computation.12 | async-start | bytes 1179648 | tf_op jit(solution)/shard_map/reduce_scatter | solution.py:46
  297.7 106.1 %all-gather.9.cloned.1.call-start = ((), (), s32[]{:S(2)}) async-start(), calls=%async_computation.13 | async-start | bytes 1179648 | tf_op jit(solution)/shard_map/all_gather | solution.py:49
  364.8 59.1 %all-reduce.9.cloned.1.call-start = ((), (), s32[]{:S(2)}) async-start(), calls=%async_computation.14 | async-start | bytes 524288 | tf_op jit(solution)/shard_map/psum | solution.py:50
  406.6 86.4 %reduce-scatter.11.cloned.1.call-start = ((), (), s32[]{:S(2)}) async-start(), calls=%async_computation.15 | async-start | bytes 1179648 | tf_op jit(solution)/shard_map/reduce_scatter | solution.py:46
  427.7 106.2 %all-gather.11.cloned.1.call-start = ((), (), s32[]{:S(2)}) async-start(), calls=%async_computation.16 | async-start | bytes 1179648 | tf_op jit(solution)/shard_map/all_gather | solution.py:49
  494.8 59.1 %all-reduce.11.cloned.1.call-start = ((), (), s32[]{:S(2)}) async-start(), calls=%async_computation.17 | async-start | bytes 524288 | tf_op jit(solution)/shard_map/psum | solution.py:50
  555.5 13.2 %all-to-all-start.1 = ((bf16[8,32,256]{2,1,0:T(8,128)(2,1)}), bf16[8,32,256]{2,1,0:T(8,128)(2,1)S(1)}, u32[]{:S(2)}, u32[]{:S(2)}) async-start(bf16[8,32,256]{2,1,0:T(8,128)(2,1)} %bitcast.27), calls=%async_computation.5 | async-start | bytes 262144 | tf_op jit(solution)/shard_map/all_to_all | solution.py:78
Sparse Core Ops, SparseCore 0:
  41.2 62.0 reduce-scatter.4
  105.5 38.5 all-gather.4
  147.0 17.1 all-reduce.4
  168.0 65.1 reduce-scatter.6
  235.3 38.5 all-gather.6
  276.8 17.1 all-reduce.6
  297.8 65.1 reduce-scatter.8
  365.3 38.5 all-gather.8
  406.7 17.1 all-reduce.8
  427.8 65.1 reduce-scatter.10
  495.3 38.5 all-gather.10
  536.7 17.1 all-reduce.10
where the time goes:
time: 577 us; the launch traced here: 576 us
  waiting for transfers between devices  407 us (71%)
  blocking collectives  101 us (18%)
  matrix products  27.1 us (5%)
  other arithmetic  15 us (3%)
  between operations  13.7 us (2%)
  starting transfers between devices  7.53 us (1%)
    reduce_scatter x4, waiting for transfers between devices, apply_layer(): summed = lax.psum_scatter(partial, 'seq', scatter_dimension=1, tiled=True)  174 us
    all_gather x4, waiting for transfers between devices, apply_layer(): hidden = lax.all_gather(hidden, 'seq', axis=1, tiled=True)  156 us
    psum x4, blocking collectives, apply_layer(): squares = lax.psum(jnp.sum(values * values, axis=1, keepdims=True), 'seq')  83.7 us
    psum x4, waiting for transfers between devices, apply_layer(): added = lax.psum(project_down(hidden, down_rows), 'mdl')  69.1 us
    all_to_all x1, blocking collectives, body(): state = lax.all_to_all(rows, 'seq', split_axis=1, concat_axis=0, tiled=True)  15.4 us
  transfers between devices with their start and end apart: 14, of which 13 were waited for; matrix products, arithmetic and copies ran while one was open for 1% of the time, Pallas kernels for 0%

commit v1 on v0

--- a/solution.py
+++ b/solution.py
@@ -6,6 +6,17 @@
 
 HOP = 128
 EPSILON = 1e-06
+
+
+def split_up(x, dim, count):
+    before, after = (x.shape[:dim], x.shape[dim + 1 :])
+    return jnp.moveaxis(x.reshape(*before, count, -1, *after), dim, 0)
+
+
+def joined_along(blocks, dim):
+    shape = list(blocks.shape[1:])
+    shape[dim] *= blocks.shape[0]
+    return jnp.moveaxis(blocks, 0, dim).reshape(shape)
 
 
 def shifted(x, axis, by):
@@ -75,7 +86,14 @@
     width = rows.shape[1]
     for layer in range(up_weight.shape[0]):
         state = apply_layer(state, up_weight[layer], down_weight[layer], width)
-    rows = lax.all_to_all(state, "seq", split_axis=0, concat_axis=1, tiled=True)
+    size_2, mine = (lax.axis_size("seq"), lax.axis_index("seq"))
+    blocks = split_up(state, 0, size_2)
+    outs = [blocks[mine]]
+    for step in range(1, size_2):
+        sent = blocks[mine ^ step]
+        outs.append(lax.ppermute(sent, "seq", [(i_2, i_2 ^ step) for i_2 in range(size_2)]))
+    blocks = jnp.stack(outs)[mine ^ jnp.arange(size_2)]
+    rows = joined_along(blocks, 1)
     full_rows = rows.reshape(streams, frames, width)
     half_streams = streams // lax.axis_size("mdl")
     return lax.dynamic_slice_in_dim(

time: 577 us -> 581 us (level)
    ppermute x0 -> x7, starting transfers between devices: none -> 11.2 us  [body(): lax.ppermute(sent, 'seq', [(i_2, i_2 ^ step) for i_2 in range(size_2)])]
    all_to_all x1 -> x0, waiting for transfers between devices: 7.45 us -> none  [body(): rows = lax.all_to_all(state, 'seq', split_axis=0, concat_axis=1, tiled=True)]
    ppermute x0 -> x7, waiting for transfers between devices: none -> 6.18 us  [body(): lax.ppermute(sent, 'seq', [(i_2, i_2 ^ step) for i_2 in range(size_2)])]
  transfers between devices with their start and end apart: 14 -> 20, of which waited for: 13 -> 15; matrix products, arithmetic and copies ran while one was open for 1% -> 1% of each run, Pallas kernels for 0% -> 0%
where the time goes in v1:
time: 581 us; the launch traced here: 580 us
  waiting for transfers between devices  405 us (70%)
  blocking collectives  101 us (17%)
  matrix products  26.9 us (5%)
  other arithmetic  14.3 us (2%)
  between operations  13.8 us (2%)
  starting transfers between devices  13 us (2%)
    reduce_scatter x4, waiting for transfers between devices, apply_layer(): summed = lax.psum_scatter(partial, 'seq', scatter_dimension=1, tiled=True)  174 us
    all_gather x4, waiting for transfers between devices, apply_layer(): hidden = lax.all_gather(hidden, 'seq', axis=1, tiled=True)  156 us
    psum x4, blocking collectives, apply_layer(): squares = lax.psum(jnp.sum(values * values, axis=1, keepdims=True), 'seq')  83.7 us
    psum x4, waiting for transfers between devices, apply_layer(): added = lax.psum(project_down(hidden, down_rows), 'mdl')  69 us
    all_to_all x1, blocking collectives, body(): state = lax.all_to_all(rows, 'seq', split_axis=1, concat_axis=0, tiled=True)  15.4 us
  transfers between devices with their start and end apart: 20, of which 15 were waited for; matrix products, arithmetic and copies ran while one was open for 1% of the time, Pallas kernels for 0%

profile of v1, /device:TPU:0, one launch (start us, length us, event | category | flops | bytes accessed | tf_op | source)
XLA Modules:
  0.0 580.3 jit_solution(3273580903190977727)
XLA Ops:
  9.5 4.7 convolution_bitcast_fusion
  22.9 15.4 %all_to_all.19 = bf16[32,8,256]{2,0,1:T(8,128)(2,1)S(1)} all-to-all(bf16[32,8,256]{2,0,1:T(8,128)(2,1)S(1)} %bitcast.117), channel_id=1, replica_groups=mesh['grp'=2,'seq'=8,'mdl'=2] {'seq'}, dimensions={1} | all-to-all | bytes 262144 | tf_op jit(solution)/shard_map/all_to_all | solution.py:85
  41.3 18.6 %psum.56 = f32[256,1]{0,1:T(1,128)S(1)} all-reduce(f32[256,1]{0,1:T(1,128)S(1)} %broadcast_in_dim.37), channel_id=1, replica_groups=mesh['grp'=2,'seq'=8,'mdl'=2] {'seq'}, use_global_device_ids=true, to_apply=%region_2.3 | all-reduce | flops 256 | bytes 2048 | tf_op jit(solution)/shard_map/psum | solution.py:55
  59.9 43.3 %reduce-scatter.5.cloned.1.call-done = bf16[256,256]{1,0:T(8,128)(2,1)} async-done(((bf16[256,2048]{1,0:T(8,128)(2,1)}), bf16[256,256]{1,0:T(8,128)(2,1)}) %reduce-scatter.5.cloned.1.call-update) | async-done | bytes 131088 | tf_op jit(solution)/shard_map/reduce_scatter | solution.py:57
  105.0 39.1 %all-gather.5.cloned.1.call-done = bf16[256,2048]{1,0:T(8,128)(2,1)} async-done(((bf16[256,256]{1,0:T(8,128)(2,1)}), bf16[256,2048]{1,0:T(8,128)(2,1)}) %all-gather.5.cloned.1.call-update) | async-done | bytes 1048592 | tf_op jit(solution)/shard_map/all_gather | solution.py:60
  144.0 2.7 fusion.14
  146.8 17.3 %all-reduce.5.cloned.1.call-done = f32[256,256]{1,0:T(8,128)} async-done(((f32[256,256]{1,0:T(8,128)}), f32[256,256]{1,0:T(8,128)}) %all-reduce.5.cloned.1.call-update) | async-done | bytes 262160 | tf_op jit(solution)/shard_map/psum | solution.py:61
  167.8 21.7 %psum.58 = f32[256,1]{0,1:T(1,128)S(1)} all-reduce(f32[256,1]{0,1:T(1,128)S(1)} %bitcast.119), channel_id=1, replica_groups=mesh['grp'=2,'seq'=8,'mdl'=2] {'seq'}, use_global_device_ids=true, to_apply=%region_6.7 | all-reduce | flops 256 | bytes 2048 | tf_op jit(solution)/shard_map/psum | solution.py:55
  189.5 43.6 %reduce-scatter.7.cloned.1.call-done = bf16[256,256]{1,0:T(8,128)(2,1)} async-done(((bf16[256,2048]{1,0:T(8,128)(2,1)}), bf16[256,256]{1,0:T(8,128)(2,1)}) %reduce-scatter.7.cloned.1.call-update) | async-done | bytes 131088 | tf_op jit(solution)/shard_map/reduce_scatter | solution.py:57
  234.9 38.8 %all-gather.7.cloned.1.call-done = bf16[256,2048]{1,0:T(8,128)(2,1)} async-done(((bf16[256,256]{1,0:T(8,128)(2,1)}), bf16[256,2048]{1,0:T(8,128)(2,1)}) %all-gather.7.cloned.1.call-update) | async-done | bytes 1048592 | tf_op jit(solution)/shard_map/all_gather | solution.py:60
  273.8 2.7 fusion.11
  276.6 17.3 %all-reduce.7.cloned.1.call-done = f32[256,256]{1,0:T(8,128)} async-done(((f32[256,256]{1,0:T(8,128)}), f32[256,256]{1,0:T(8,128)}) %all-reduce.7.cloned.1.call-update) | async-done | bytes 262160 | tf_op jit(solution)/shard_map/psum | solution.py:61
  297.6 21.7 %psum.60 = f32[256,1]{0,1:T(1,128)S(1)} all-reduce(f32[256,1]{0,1:T(1,128)S(1)} %bitcast.120), channel_id=1, replica_groups=mesh['grp'=2,'seq'=8,'mdl'=2] {'seq'}, use_global_device_ids=true, to_apply=%region_10.11 | all-reduce | flops 256 | bytes 2048 | tf_op jit(solution)/shard_map/psum | solution.py:55
  319.3 43.6 %reduce-scatter.9.cloned.1.call-done = bf16[256,256]{1,0:T(8,128)(2,1)} async-done(((bf16[256,2048]{1,0:T(8,128)(2,1)}), bf16[256,256]{1,0:T(8,128)(2,1)}) %reduce-scatter.9.cloned.1.call-update) | async-done | bytes 131088 | tf_op jit(solution)/shard_map/reduce_scatter | solution.py:57
  364.7 39.0 %all-gather.9.cloned.1.call-done = bf16[256,2048]{1,0:T(8,128)(2,1)} async-done(((bf16[256,256]{1,0:T(8,128)(2,1)}), bf16[256,2048]{1,0:T(8,128)(2,1)}) %all-gather.9.cloned.1.call-update) | async-done | bytes 1048592 | tf_op jit(solution)/shard_map/all_gather | solution.py:60
  403.7 2.7 fusion.8
  406.5 17.3 %all-reduce.9.cloned.1.call-done = f32[256,256]{1,0:T(8,128)} async-done(((f32[256,256]{1,0:T(8,128)}), f32[256,256]{1,0:T(8,128)}) %all-reduce.9.cloned.1.call-update) | async-done | bytes 262160 | tf_op jit(solution)/shard_map/psum | solution.py:61
  427.5 21.7 %psum.62 = f32[256,1]{0,1:T(1,128)S(1)} all-reduce(f32[256,1]{0,1:T(1,128)S(1)} %bitcast.121), channel_id=1, replica_groups=mesh['grp'=2,'seq'=8,'mdl'=2] {'seq'}, use_global_device_ids=true, to_apply=%region_14.15 | all-reduce | flops 256 | bytes 2048 | tf_op jit(solution)/shard_map/psum | solution.py:55
  449.2 43.6 %reduce-scatter.11.cloned.1.call-done = bf16[256,256]{1,0:T(8,128)(2,1)} async-done(((bf16[256,2048]{1,0:T(8,128)(2,1)}), bf16[256,256]{1,0:T(8,128)(2,1)}) %reduce-scatter.11.cloned.1.call-update) | async-done | bytes 131088 | tf_op jit(solution)/shard_map/reduce_scatter | solution.py:57
  494.6 39.0 %all-gather.11.cloned.1.call-done = bf16[256,2048]{1,0:T(8,128)(2,1)} async-done(((bf16[256,256]{1,0:T(8,128)(2,1)}), bf16[256,2048]{1,0:T(8,128)(2,1)}) %all-gather.11.cloned.1.call-update) | async-done | bytes 1048592 | tf_op jit(solution)/shard_map/all_gather | solution.py:60
  533.6 2.7 fusion.5
  536.4 17.2 %all-reduce.11.cloned.1.call-done = f32[256,256]{1,0:T(8,128)} async-done(((f32[256,256]{1,0:T(8,128)}), f32[256,256]{1,0:T(8,128)}) %all-reduce.11.cloned.1.call-update) | async-done | bytes 262160 | tf_op jit(solution)/shard_map/psum | solution.py:61
  562.3 3.3 collective-permute-start.6
  567.8 4.2 collective-permute-done.7
  (97 shorter events, 45.3 us)
Async XLA Ops:
  6.5 12.9 %copy-start = (bf16[64,128,16]{1,2,0:T(8,128)(2,1)S(1)}, bf16[64,128,16]{1,2,0:T(8,128)(2,1)}, u32[]{:S(2)}) copy-start(bf16[64,128,16]{1,2,0:T(8,128)(2,1)} %param.7) | copy-start | bytes 786436
  6.5 96.6 %reduce-scatter.5.cloned.1.call-start = ((), (), s32[]{:S(2)}) async-start(), calls=%async_computation.5 | async-start | bytes 1179648 | tf_op jit(solution)/shard_map/reduce_scatter | solution.py:57
  7.5 9.2 %collective-permute-start = (f32[4,64,128]{2,1,0:T(8,128)S(1)}, f32[4,64,128]{2,1,0:T(8,128)S(1)}, u32[]{:S(2)}, u32[]{:S(2)}) collective-permute-start(f32[4,64,128]{2,1,0:T(8,128)S(1)} %slice.49), channel_id=1, source_target_pairs={{2,0},{4,2},{6,4},{8,6},{10,8},{12,10},{14,12},{3,1},{5,3},{7,5},{... | collective-permute-start | bytes 393224 | tf_op jit(solution)/shard_map/ppermute | solution.py:25
  9.5 7.0 %copy-start.2 = (s32[4]{0:T(128)S(1)}, s32[4]{0:T(128)}, u32[]{:S(2)}) copy-start(s32[4]{0:T(128)} %param.6) | copy-start | bytes 52
  14.3 1.9 copy-start.1
  41.0 103.0 %all-gather.5.cloned.1.call-start = ((), (), s32[]{:S(2)}) async-start(), calls=%async_computation.6 | async-start | bytes 1179648 | tf_op jit(solution)/shard_map/all_gather | solution.py:60
  104.9 59.2 %all-reduce.5.cloned.1.call-start = ((), (), s32[]{:S(2)}) async-start(), calls=%async_computation.7 | async-start | bytes 524288 | tf_op jit(solution)/shard_map/psum | solution.py:61
  146.8 86.4 %reduce-scatter.7.cloned.1.call-start = ((), (), s32[]{:S(2)}) async-start(), calls=%async_computation.8 | async-start | bytes 1179648 | tf_op jit(solution)/shard_map/reduce_scatter | solution.py:57
  167.8 106.0 %all-gather.7.cloned.1.call-start = ((), (), s32[]{:S(2)}) async-start(), calls=%async_computation.9 | async-start | bytes 1179648 | tf_op jit(solution)/shard_map/all_gather | solution.py:60
  234.9 58.9 %all-reduce.7.cloned.1.call-start = ((), (), s32[]{:S(2)}) async-start(), calls=%async_computation.10 | async-start | bytes 524288 | tf_op jit(solution)/shard_map/psum | solution.py:61
  276.5 86.4 %reduce-scatter.9.cloned.1.call-start = ((), (), s32[]{:S(2)}) async-start(), calls=%async_computation.11 | async-start | bytes 1179648 | tf_op jit(solution)/shard_map/reduce_scatter | solution.py:57
  297.5 106.1 %all-gather.9.cloned.1.call-start = ((), (), s32[]{:S(2)}) async-start(), calls=%async_computation.12 | async-start | bytes 1179648 | tf_op jit(solution)/shard_map/all_gather | solution.py:60
  364.6 59.1 %all-reduce.9.cloned.1.call-start = ((), (), s32[]{:S(2)}) async-start(), calls=%async_computation.13 | async-start | bytes 524288 | tf_op jit(solution)/shard_map/psum | solution.py:61
  406.4 86.4 %reduce-scatter.11.cloned.1.call-start = ((), (), s32[]{:S(2)}) async-start(), calls=%async_computation.14 | async-start | bytes 1179648 | tf_op jit(solution)/shard_map/reduce_scatter | solution.py:57
  427.4 106.1 %all-gather.11.cloned.1.call-start = ((), (), s32[]{:S(2)}) async-start(), calls=%async_computation.15 | async-start | bytes 1179648 | tf_op jit(solution)/shard_map/all_gather | solution.py:60
  494.5 59.1 %all-reduce.11.cloned.1.call-start = ((), (), s32[]{:S(2)}) async-start(), calls=%async_computation.16 | async-start | bytes 524288 | tf_op jit(solution)/shard_map/psum | solution.py:61
  554.6 7.7 %collective-permute-start.1 = (bf16[32,256]{1,0:T(8,128)(2,1)S(1)}, bf16[32,256]{1,0:T(8,128)(2,1)S(1)}, u32[]{:S(2)}, u32[]{:S(2)}) collective-permute-start(bf16[32,256]{1,0:T(8,128)(2,1)S(1)} %get-tuple-element.19), channel_id=1, source_target_pairs={{0,2},{2,0},{4,6},{6,4},{8,10},{10,8},{12,14},{14,12},{1,3},{3,1},... | collective-permute-start | bytes 49160 | tf_op jit(solution)/shard_map/ppermute | solution.py:94
  556.4 9.2 %collective-permute-start.2 = (bf16[32,256]{1,0:T(8,128)(2,1)S(1)}, bf16[32,256]{1,0:T(8,128)(2,1)S(1)}, u32[]{:S(2)}, u32[]{:S(2)}) collective-permute-start(bf16[32,256]{1,0:T(8,128)(2,1)S(1)} %get-tuple-element.18), channel_id=1, source_target_pairs={{0,4},{2,6},{4,0},{6,2},{8,12},{10,14},{12,8},{14,10},{1,5},{3,7},... | collective-permute-start | bytes 49160 | tf_op jit(solution)/shard_map/ppermute | solution.py:94
  557.9 7.9 %collective-permute-start.3 = (bf16[32,256]{1,0:T(8,128)(2,1)S(1)}, bf16[32,256]{1,0:T(8,128)(2,1)S(1)}, u32[]{:S(2)}, u32[]{:S(2)}) collective-permute-start(bf16[32,256]{1,0:T(8,128)(2,1)S(1)} %get-tuple-element.17), channel_id=1, source_target_pairs={{0,6},{2,4},{4,2},{6,0},{8,14},{10,12},{12,10},{14,8},{1,7},{3,5},... | collective-permute-start | bytes 49160 | tf_op jit(solution)/shard_map/ppermute | solution.py:94
  558.2 7.7 %collective-permute-start.4 = (bf16[32,256]{1,0:T(8,128)(2,1)S(1)}, bf16[32,256]{1,0:T(8,128)(2,1)S(1)}, u32[]{:S(2)}, u32[]{:S(2)}) collective-permute-start(bf16[32,256]{1,0:T(8,128)(2,1)S(1)} %get-tuple-element.16), channel_id=1, source_target_pairs={{0,8},{2,10},{4,12},{6,14},{8,0},{10,2},{12,4},{14,6},{1,9},{3,11}... | collective-permute-start | bytes 49160 | tf_op jit(solution)/shard_map/ppermute | solution.py:94
  560.9 5.5 collective-permute-start.5
  562.3 5.5 collective-permute-start.6
  565.6 6.4 %collective-permute-start.7 = (bf16[32,256]{1,0:T(8,128)(2,1)S(1)}, bf16[32,256]{1,0:T(8,128)(2,1)S(1)}, u32[]{:S(2)}, u32[]{:S(2)}) collective-permute-start(bf16[32,256]{1,0:T(8,128)(2,1)S(1)} %get-tuple-element.13), channel_id=1, source_target_pairs={{0,14},{2,12},{4,10},{6,8},{8,6},{10,4},{12,2},{14,0},{1,15},{3,13... | collective-permute-start | bytes 49160 | tf_op jit(solution)/shard_map/ppermute | solution.py:94
Sparse Core Ops, SparseCore 0:
  41.2 61.9 reduce-scatter.4
  105.4 38.5 all-gather.4
  146.9 17.1 all-reduce.4
  167.9 65.1 reduce-scatter.6
  235.2 38.5 all-gather.6
  276.6 17.1 all-reduce.6
  297.7 65.1 reduce-scatter.8
  365.1 38.5 all-gather.8
  406.5 17.1 all-reduce.8
  427.6 65.1 reduce-scatter.10
  495.0 38.5 all-gather.10
  536.4 17.1 all-reduce.10
